TPU v7x, 128 devices: a whole 4x4x4 slice. The times are simulated.
128 devices in a mesh: dom: 16 (over y, z), sub: 8 (over x, core).
Axes of the slice: x: 4, y: 4, z: 4, core: 2. Of those that a mesh axis runs over, the one named last changes fastest.
Arguments:
- features: bfloat16 [131072, 256], P(('dom', 'sub')), may hold values from -6 to 6
- cotangent: bfloat16 [131072, 256], P(('dom', 'sub')), may hold values from -6 to 6
- w_self_one: bfloat16 [256, 256], replicated, may hold values from -0.375 to 0.375
- w_nbr_one: bfloat16 [256, 256], replicated, may hold values from -0.375 to 0.375
- bias_one: float32 [256], replicated, may hold values from -4 to 4
- w_self_two: bfloat16 [256, 256], replicated, may hold values from -0.375 to 0.375
- w_nbr_two: bfloat16 [256, 256], replicated, may hold values from -0.375 to 0.375
- in_count: int32 [131072], P(('dom', 'sub')), may hold values from 0 to 7
- send_list: int32 [128, 128, 4], P(('dom', 'sub')), may hold values from 0 to 1023
- src_slot: int32 [128, 2048], P(('dom', 'sub')), may hold values from 0 to 1535
- dst_slot: int32 [128, 2048], P(('dom', 'sub')), may hold values from 0 to 1535
- edge_count: int32 [128], P(('dom', 'sub')), may hold values from 512 to 2048, as said below
Outputs:
- grad_features: bfloat16 [131072, 256], P(('dom', 'sub'))
- grad_weights: float32 [4, 256, 256], replicated
- grad_bias: float32 [256], replicated
Inputs may be any that keep to these rules, and one draw needn't show every extreme that they name: Each device's first edge_count slots are live; one device has all 2048 live in every draw.
All inputs are finite; a program needn't handle non-finite values.
Results may differ from a plain program's by a relative error of at most 0.0056.
Values may be sent and summed in bfloat16 or wider, within the bound.
A program may use at most 64 MiB of HBM per device.

v0:
```python
import math
import jax
import jax.numpy as jnp
from jax import lax
from jax.sharding import PartitionSpec as P


def to_mirrors(master_rows, send_list):
    picked_rows = jnp.take(master_rows, send_list[0], axis=0)
    feature_dim = master_rows.shape[1]
    received = lax.all_to_all(picked_rows, ("dom", "sub"), split_axis=0, concat_axis=0, tiled=True)
    return received.reshape(-1, feature_dim)


def to_masters(mirror_partial, send_list, node_dev):
    feature_dim = mirror_partial.shape[1]
    per_peer = send_list.shape[2]
    sectioned_rows = mirror_partial.reshape(-1, per_peer, feature_dim)
    received = lax.all_to_all(
        sectioned_rows, ("dom", "sub"), split_axis=0, concat_axis=0, tiled=True
    )
    flat_rows = received.reshape(-1, feature_dim)
    owners = send_list[0].reshape(-1)
    placing = (jnp.arange(node_dev, dtype=jnp.int32)[:, None] == owners[None, :]).astype(
        jnp.float32
    )
    return jnp.dot(
        placing, flat_rows, precision=lax.Precision.HIGHEST, preferred_element_type=jnp.float32
    )


def spread(slot_table, from_slot, into_slot, live_count):
    slot_total = slot_table.shape[0]
    edge_slots = from_slot.shape[0]
    feature_dim = slot_table.shape[1]
    block_rows = math.gcd(512, edge_slots)
    slot_ids = jnp.arange(slot_total, dtype=jnp.int32)[None, :]

    def one_block(turn_index, total):
        offset = turn_index * block_rows
        from_part = lax.dynamic_slice_in_dim(from_slot, offset, block_rows)
        into_part = lax.dynamic_slice_in_dim(into_slot, offset, block_rows)
        live_rows = (jnp.arange(block_rows, dtype=jnp.int32) + offset < live_count)[:, None]
        picking = ((from_part[:, None] == slot_ids) & live_rows).astype(slot_table.dtype)
        picked_rows = jnp.dot(picking, slot_table, preferred_element_type=jnp.float32).astype(
            slot_table.dtype
        )
        placing = (into_part[:, None] == slot_ids).astype(slot_table.dtype)
        return total + tdot(placing, picked_rows)

    start_total = jnp.zeros((slot_total, feature_dim), jnp.float32)
    block_count = edge_slots // block_rows
    return lax.fori_loop(0, block_count, one_block, start_total)


def tdot(left, right):
    return lax.dot_general(
        left, right, (((0,), (0,)), ((), ())), preferred_element_type=jnp.float32
    )


def dot_transposed(left, right):
    return lax.dot_general(
        left, right, (((1,), (1,)), ((), ())), preferred_element_type=jnp.float32
    )


def silu_grad(value):
    sigmoid_v = jax.nn.sigmoid(value)
    return sigmoid_v * (1.0 + value * (1.0 - sigmoid_v))


def shards(
    features,
    cotangent,
    w_self_one,
    w_nbr_one,
    bias_one,
    w_self_two,
    w_nbr_two,
    in_count,
    send_list,
    src_slot,
    dst_slot,
    edge_count,
):
    node_dev = features.shape[0]
    sources = src_slot[0]
    targets = dst_slot[0]
    live_count = edge_count[0]
    inverse = (1.0 / jnp.maximum(in_count, 1).astype(jnp.float32))[:, None]

    def gather_sum(master_rows, from_slot, into_slot):
        slot_table = jnp.concatenate([master_rows, to_mirrors(master_rows, send_list)], axis=0)
        partial_value = spread(slot_table, from_slot, into_slot, live_count)
        return partial_value[:node_dev] + to_masters(partial_value[node_dev:], send_list, node_dev)

    mean_one = (gather_sum(features, sources, targets) * inverse).astype(jnp.bfloat16)
    z_one = (
        jnp.dot(features, w_self_one, preferred_element_type=jnp.float32)
        + jnp.dot(mean_one, w_nbr_one, preferred_element_type=jnp.float32)
        + bias_one
    )
    h_one = jax.nn.silu(z_one).astype(jnp.bfloat16)
    message_two = (dot_transposed(cotangent, w_nbr_two) * inverse).astype(jnp.bfloat16)
    forward_sum = gather_sum(h_one, sources, targets)
    backward_sum = gather_sum(message_two, targets, sources)
    mean_two = (forward_sum * inverse).astype(jnp.bfloat16)
    late_self = tdot(h_one, cotangent)
    late_nbr = tdot(mean_two, cotangent)
    grad_h_one = dot_transposed(cotangent, w_self_two) + backward_sum
    grad_z_one = (grad_h_one * silu_grad(z_one)).astype(jnp.bfloat16)
    message_one = (dot_transposed(grad_z_one, w_nbr_one) * inverse).astype(jnp.bfloat16)
    early_self = tdot(features, grad_z_one)
    early_nbr = tdot(mean_one, grad_z_one)
    early_bias = jnp.sum(grad_z_one.astype(jnp.float32), axis=0)
    grad_features = (
        dot_transposed(grad_z_one, w_self_one) + gather_sum(message_one, targets, sources)
    ).astype(jnp.bfloat16)
    self_one, nbr_one, bias_sum, self_two, nbr_two = lax.psum(
        (early_self, early_nbr, early_bias, late_self, late_nbr), ("dom", "sub")
    )
    norm_factor = jnp.float32(node_dev * lax.axis_size("dom") * lax.axis_size("sub")) ** (-0.5)
    grad_weights = jnp.stack([self_one, nbr_one, self_two, nbr_two]) * norm_factor
    grad_bias = bias_sum * norm_factor
    return (grad_features, grad_weights, grad_bias)


def solution(mesh):
    return jax.shard_map(
        shards,
        mesh=mesh,
        in_specs=(
            P(("dom", "sub"), None),
            P(("dom", "sub"), None),
            P(),
            P(),
            P(),
            P(),
            P(),
            P(("dom", "sub")),
            P(("dom", "sub"), None, None),
            P(("dom", "sub"), None),
            P(("dom", "sub"), None),
            P(("dom", "sub")),
        ),
        out_specs=(P(("dom", "sub"), None), P(), P()),
        check_vma=False,
    )
```

profile of v0, /device:TPU:1, one launch (start us, length us, event | category | flops | bytes accessed | tf_op | source)
XLA Modules:
  0.0 453.2 jit_solution(3980596526978102994)
XLA Ops:
  16.2 11.9 %all-to-all-start = ((bf16[128,4,256]{2,1,0:T(4,128)(2,1)}), bf16[128,4,256]{2,1,0:T(4,128)(2,1)}, u32[]{:S(2)}, u32[]{:S(2)}) async-start(bf16[128,4,256]{2,1,0:T(4,128)(2,1)} %get-tuple-element.741), calls=%async_computation | async-start | bytes 524288 | tf_op jit(solution)/shard_map/all_to_all | solution.py:11
  29.0 9.7 %all-to-all-done = bf16[128,4,256]{2,1,0:T(4,128)(2,1)} async-done(((bf16[128,4,256]{2,1,0:T(4,128)(2,1)}), bf16[128,4,256]{2,1,0:T(4,128)(2,1)}, u32[]{:S(2)}, u32[]{:S(2)}) %all-to-all-start) | async-done | bytes 262176 | tf_op jit(solution)/shard_map/all_to_all | solution.py:11
  38.7 4.6 %all-to-all-start.2 = ((bf16[128,4,256]{2,1,0:T(4,128)(2,1)}), bf16[128,4,256]{2,1,0:T(4,128)(2,1)S(1)}, u32[]{:S(2)}, u32[]{:S(2)}) async-start(bf16[128,4,256]{2,1,0:T(4,128)(2,1)} %get-tuple-element.740), calls=%async_computation.2 | async-start | bytes 524288 | tf_op jit(solution)/shard_map/all_to_all | solution.py:11
  46.9 20.3 %while.60 = (s32[]{:T(128)}, f32[1536,256]{1,0:T(8,128)S(1)}, s32[2048]{0:T(1024)S(1)}, s32[2048]{0:T(1024)}, s32[]{:T(128)}, /*index=5*/bf16[1536,256]{1,0:T(8,...) while((s32[]{:T(128)}, f32[1536,256]{1,0:T(8,128)S(1)}, s32[2048]{0:T(1024)S(1)}, ...), condition=%wide.region_1.3_spmd.clone.clone, body=%wide.region_0.0_spmd.clone.clone.sunk | while | flops 808584192 | bytes 3945645 | solution.py:53
  48.4 3.6 fusion.125
  53.5 3.6 fusion.125
  58.6 3.6 fusion.125
  63.7 3.6 fusion.125
  68.7 9.8 %all-to-all-start.1 = ((f32[128,4,256]{2,1,0:T(4,128)}), f32[128,4,256]{2,1,0:T(4,128)S(1)}, u32[]{:S(2)}, u32[]{:S(2)}) async-start(f32[128,4,256]{2,1,0:T(4,128)} %reshape.79), calls=%async_computation.1 | async-start | bytes 1048576 | tf_op jit(solution)/shard_map/all_to_all | solution.py:19
  78.6 22.6 %while.61 = (s32[]{:T(128)}, f32[1536,256]{1,0:T(8,128)}, s32[2048]{0:T(1024)}, s32[2048]{0:T(1024)S(1)}, s32[]{:T(128)}, /*index=5*/bf16[1536,256]{1,0:T(8,128)...) while((s32[]{:T(128)}, f32[1536,256]{1,0:T(8,128)}, s32[2048]{0:T(1024)}, ...), condition=%wide.region_3.5_spmd.clone.clone, body=%wide.region_2.4_spmd.clone.clone.sunk | while | flops 808584192 | bytes 3945645 | solution.py:53
  84.7 4.5 fusion.128
  90.7 4.5 fusion.128
  96.7 4.5 fusion.128
  103.2 9.8 %all-to-all-start.3 = ((f32[128,4,256]{2,1,0:T(4,128)}), f32[128,4,256]{2,1,0:T(4,128)S(1)}, u32[]{:S(2)}, u32[]{:S(2)}) async-start(f32[128,4,256]{2,1,0:T(4,128)} %reshape.82), calls=%async_computation.3 | async-start | bytes 1048576 | tf_op jit(solution)/shard_map/all_to_all | solution.py:19
  117.8 8.8 %all-to-all-done.3 = f32[128,4,256]{2,1,0:T(4,128)S(1)} async-done(((f32[128,4,256]{2,1,0:T(4,128)}), f32[128,4,256]{2,1,0:T(4,128)S(1)}, u32[]{:S(2)}, u32[]{:S(2)}) %all-to-all-start.3) | async-done | bytes 524320 | tf_op jit(solution)/shard_map/all_to_all | solution.py:19
  139.1 4.6 %all-to-all-start.6 = ((bf16[128,4,256]{2,1,0:T(4,128)(2,1)}), bf16[128,4,256]{2,1,0:T(4,128)(2,1)S(1)}, u32[]{:S(2)}, u32[]{:S(2)}) async-start(bf16[128,4,256]{2,1,0:T(4,128)(2,1)} %get-tuple-element.738), calls=%async_computation.6 | async-start | bytes 524288 | tf_op jit(solution)/shard_map/all_to_all | solution.py:11
  144.8 67.1 %psum.39 = f32[256]{0:T(256)S(1)} all-reduce(f32[256]{0:T(256)S(1)} %copy-done.15), channel_id=1, replica_groups=mesh['dom'=16,'sub'=8] {'dom','sub'}, use_global_device_ids=true, to_apply=%region_13.15 | all-reduce | flops 256 | bytes 2048 | tf_op jit(solution)/shard_map/psum | solution.py:120
  212.5 4.7 %all-to-all-start.4 = ((bf16[128,4,256]{2,1,0:T(4,128)(2,1)}), bf16[128,4,256]{2,1,0:T(4,128)(2,1)S(1)}, u32[]{:S(2)}, u32[]{:S(2)}) async-start(bf16[128,4,256]{2,1,0:T(4,128)(2,1)} %get-tuple-element.739), calls=%async_computation.4 | async-start | bytes 524288 | tf_op jit(solution)/shard_map/all_to_all | solution.py:11
  218.2 21.7 %while.63 = (s32[]{:T(128)}, f32[1536,256]{1,0:T(8,128)}, s32[2048]{0:T(1024)S(1)}, s32[2048]{0:T(1024)S(1)}, s32[]{:T(128)}, /*index=5*/bf16[1536,256]{1,0:T(8,...) while((s32[]{:T(128)}, f32[1536,256]{1,0:T(8,128)}, s32[2048]{0:T(1024)S(1)}, ...), condition=%wide.region_10.12_spmd.clone.clone, body=%wide.region_9.11_spmd.clone.clone.sunk | while | flops 808584192 | bytes 3945645 | solution.py:53
  219.0 4.2 fusion.134
  224.0 4.7 %fusion.134 = f32[1536,256]{1,0:T(8,128)} fusion(f32[1536,256]{1,0:T(8,128)} %get-tuple-element.995, s32[512]{0:T(512)S(1)} %dynamic_slice.86, bf16[1536,256]{1,0:T(8,128)(2,1)} %get-tuple-element.1009, s32[512]{0:T(512)S(1)} %dynamic_slice.87, pred[512]{0:T(512)(128)(4,1)S(1)} %add_compare_fusion.11, pred[]{:T(512)S(6)} %compare.15), kind=kOutput, calls=%fused_computation.46.clone.1 | convolution fusion | flops 808583168 | bytes 3936769 | tf_op jit(solution)/shard_map/while/body/eval_jaxpr/dot_general | solution.py:57
  229.6 4.7 %fusion.134 = f32[1536,256]{1,0:T(8,128)} fusion(f32[1536,256]{1,0:T(8,128)} %get-tuple-element.995, s32[512]{0:T(512)S(1)} %dynamic_slice.86, bf16[1536,256]{1,0:T(8,128)(2,1)} %get-tuple-element.1009, s32[512]{0:T(512)S(1)} %dynamic_slice.87, pred[512]{0:T(512)(128)(4,1)S(1)} %add_compare_fusion.11, pred[]{:T(512)S(6)} %compare.15), kind=kOutput, calls=%fused_computation.46.clone.1 | convolution fusion | flops 808583168 | bytes 3936769 | tf_op jit(solution)/shard_map/while/body/eval_jaxpr/dot_general | solution.py:57
  235.1 4.7 %fusion.134 = f32[1536,256]{1,0:T(8,128)} fusion(f32[1536,256]{1,0:T(8,128)} %get-tuple-element.995, s32[512]{0:T(512)S(1)} %dynamic_slice.86, bf16[1536,256]{1,0:T(8,128)(2,1)} %get-tuple-element.1009, s32[512]{0:T(512)S(1)} %dynamic_slice.87, pred[512]{0:T(512)(128)(4,1)S(1)} %add_compare_fusion.11, pred[]{:T(512)S(6)} %compare.15), kind=kOutput, calls=%fused_computation.46.clone.1 | convolution fusion | flops 808583168 | bytes 3936769 | tf_op jit(solution)/shard_map/while/body/eval_jaxpr/dot_general | solution.py:57
  241.9 9.8 %all-to-all-start.7 = ((f32[128,4,256]{2,1,0:T(4,128)}), f32[128,4,256]{2,1,0:T(4,128)S(1)}, u32[]{:S(2)}, u32[]{:S(2)}) async-start(f32[128,4,256]{2,1,0:T(4,128)} %reshape.88), calls=%async_computation.7 | async-start | bytes 1048576 | tf_op jit(solution)/shard_map/all_to_all | solution.py:19
  252.7 21.8 %while.62 = (s32[]{:T(128)}, f32[1536,256]{1,0:T(8,128)}, s32[2048]{0:T(1024)S(1)}, s32[2048]{0:T(1024)S(1)}, s32[]{:T(128)}, /*index=5*/bf16[1536,256]{1,0:T(8,...) while((s32[]{:T(128)}, f32[1536,256]{1,0:T(8,128)}, s32[2048]{0:T(1024)S(1)}, ...), condition=%wide.region_5.7_spmd.clone.clone, body=%wide.region_4.6_spmd.clone.clone.sunk | while | flops 808584192 | bytes 3945645 | solution.py:53
  253.5 4.3 fusion.131
  258.6 4.8 %fusion.131 = f32[1536,256]{1,0:T(8,128)} fusion(f32[1536,256]{1,0:T(8,128)} %get-tuple-element.965, s32[512]{0:T(512)S(1)} %dynamic_slice.84, bf16[1536,256]{1,0:T(8,128)(2,1)} %get-tuple-element.979, s32[512]{0:T(512)S(1)} %dynamic_slice.85, pred[512]{0:T(512)(128)(4,1)S(1)} %add_compare_fusion.10, pred[]{:T(512)S(6)} %compare.14), kind=kOutput, calls=%fused_computation.35.clone.1 | convolution fusion | flops 808583168 | bytes 3936769 | tf_op jit(solution)/shard_map/while/body/eval_jaxpr/dot_general | solution.py:57
  264.1 4.8 %fusion.131 = f32[1536,256]{1,0:T(8,128)} fusion(f32[1536,256]{1,0:T(8,128)} %get-tuple-element.965, s32[512]{0:T(512)S(1)} %dynamic_slice.84, bf16[1536,256]{1,0:T(8,128)(2,1)} %get-tuple-element.979, s32[512]{0:T(512)S(1)} %dynamic_slice.85, pred[512]{0:T(512)(128)(4,1)S(1)} %add_compare_fusion.10, pred[]{:T(512)S(6)} %compare.14), kind=kOutput, calls=%fused_computation.35.clone.1 | convolution fusion | flops 808583168 | bytes 3936769 | tf_op jit(solution)/shard_map/while/body/eval_jaxpr/dot_general | solution.py:57
  269.7 4.8 %fusion.131 = f32[1536,256]{1,0:T(8,128)} fusion(f32[1536,256]{1,0:T(8,128)} %get-tuple-element.965, s32[512]{0:T(512)S(1)} %dynamic_slice.84, bf16[1536,256]{1,0:T(8,128)(2,1)} %get-tuple-element.979, s32[512]{0:T(512)S(1)} %dynamic_slice.85, pred[512]{0:T(512)(128)(4,1)S(1)} %add_compare_fusion.10, pred[]{:T(512)S(6)} %compare.14), kind=kOutput, calls=%fused_computation.35.clone.1 | convolution fusion | flops 808583168 | bytes 3936769 | tf_op jit(solution)/shard_map/while/body/eval_jaxpr/dot_general | solution.py:57
  276.5 9.8 %all-to-all-start.5 = ((f32[128,4,256]{2,1,0:T(4,128)}), f32[128,4,256]{2,1,0:T(4,128)S(1)}, u32[]{:S(2)}, u32[]{:S(2)}) async-start(f32[128,4,256]{2,1,0:T(4,128)} %reshape.85), calls=%async_computation.5 | async-start | bytes 1048576 | tf_op jit(solution)/shard_map/all_to_all | solution.py:19
  291.0 8.9 %all-to-all-done.5 = f32[128,4,256]{2,1,0:T(4,128)S(1)} async-done(((f32[128,4,256]{2,1,0:T(4,128)}), f32[128,4,256]{2,1,0:T(4,128)S(1)}, u32[]{:S(2)}, u32[]{:S(2)}) %all-to-all-start.5) | async-done | bytes 524320 | tf_op jit(solution)/shard_map/all_to_all | solution.py:19
  303.5 140.2 %all-reduce.3.cloned.1.call-done = (f32[1,256,256]{1,2,0:T(8,128)}, f32[1,256,256]{1,2,0:T(8,128)}, f32[1,256,256]{1,2,0:T(8,128)}, f32[1,256,256]{1,2,0:T(8,128)}) async-done(((f32[1,256,256]{1,2,0:T(8,128)}, f32[1,256,256]{1,2,0:T(8,128)}, f32[1,256,256]{1,2,0:T(8,128)}, f32[1,256,256]{1,2,0:T(8,128)}), (f32[1,256,256]{1,2,0:T(8,128)}, f32[1,256,256]{1,2,0:T(8,128)}, f32[1,256,256]{1,2,0:T(8,128)}, ...) | async-done | bytes 1048592 | tf_op jit(solution)/shard_map/psum | solution.py:120
  (150 shorter events, 74.0 us)
Async XLA Ops:
  7.2 2.4 copy-start
  10.8 2.0 copy-start.1
  14.8 13.4 %copy-start.12 = (s32[1,128,4]{1,2,0:T(4,128)S(1)}, s32[1,128,4]{1,2,0:T(4,128)}, u32[]{:S(2)}) copy-start(s32[1,128,4]{1,2,0:T(4,128)} %param.30) | copy-start | bytes 6148
  15.0 1.2 copy-start.10
  16.2 30.7 %copy-start.8 = (s32[1,2048]{1,0:T(1,128)S(1)}, s32[1,2048]{1,0:T(1,128)}, u32[]{:S(2)}) copy-start(s32[1,2048]{1,0:T(1,128)} %param.31) | copy-start | bytes 24580
  16.2 22.5 %all-to-all-start = ((bf16[128,4,256]{2,1,0:T(4,128)(2,1)}), bf16[128,4,256]{2,1,0:T(4,128)(2,1)}, u32[]{:S(2)}, u32[]{:S(2)}) async-start(bf16[128,4,256]{2,1,0:T(4,128)(2,1)} %get-tuple-element.741), calls=%async_computation | async-start | bytes 524288 | tf_op jit(solution)/shard_map/all_to_all | solution.py:11
  38.7 29.8 %all-to-all-start.2 = ((bf16[128,4,256]{2,1,0:T(4,128)(2,1)}), bf16[128,4,256]{2,1,0:T(4,128)(2,1)S(1)}, u32[]{:S(2)}, u32[]{:S(2)}) async-start(bf16[128,4,256]{2,1,0:T(4,128)(2,1)} %get-tuple-element.740), calls=%async_computation.2 | async-start | bytes 524288 | tf_op jit(solution)/shard_map/all_to_all | solution.py:11
  67.3 1.4 copy-start.2
  68.7 34.5 %all-to-all-start.1 = ((f32[128,4,256]{2,1,0:T(4,128)}), f32[128,4,256]{2,1,0:T(4,128)S(1)}, u32[]{:S(2)}, u32[]{:S(2)}) async-start(f32[128,4,256]{2,1,0:T(4,128)} %reshape.79), calls=%async_computation.1 | async-start | bytes 1048576 | tf_op jit(solution)/shard_map/all_to_all | solution.py:19
  101.2 11.8 %copy-start.7 = (bf16[256,256]{1,0:T(8,128)(2,1)S(1)}, bf16[256,256]{1,0:T(8,128)(2,1)}, u32[]{:S(2)}) copy-start(bf16[256,256]{1,0:T(8,128)(2,1)} %param.24) | copy-start | bytes 393220
  103.2 23.4 %all-to-all-start.3 = ((f32[128,4,256]{2,1,0:T(4,128)}), f32[128,4,256]{2,1,0:T(4,128)S(1)}, u32[]{:S(2)}, u32[]{:S(2)}) async-start(f32[128,4,256]{2,1,0:T(4,128)} %reshape.82), calls=%async_computation.3 | async-start | bytes 1048576 | tf_op jit(solution)/shard_map/all_to_all | solution.py:19
  113.0 1.5 copy-start.13
  117.8 11.3 %copy-start.4 = (f32[1024,256]{1,0:T(8,128)S(1)}, f32[1024,256]{1,0:T(8,128)}, u32[]{:S(2)}) copy-start(f32[1024,256]{1,0:T(8,128)} %fusion.82) | copy-start | bytes 3145732
  117.8 11.4 %copy-start.11 = (bf16[256,256]{1,0:T(8,128)(2,1)S(1)}, bf16[256,256]{1,0:T(8,128)(2,1)}, u32[]{:S(2)}) copy-start(bf16[256,256]{1,0:T(8,128)(2,1)} %param.25) | copy-start | bytes 393220
  129.2 1.3 copy-start.5
  129.2 1.4 copy-start.3
  129.2 1.4 copy-start.16
  137.1 6.6 %copy-start.6 = (bf16[1024,256]{1,0:T(8,128)(2,1)S(1)}, bf16[1024,256]{1,0:T(8,128)(2,1)}, u32[]{:S(2)}) copy-start(bf16[1024,256]{1,0:T(8,128)(2,1)} %copy-done.5) | copy-start | bytes 1572868
  137.2 7.6 %copy-start.15 = (f32[256]{0:T(256)S(1)}, f32[256]{0:T(256)}, u32[]{:S(2)}) copy-start(f32[256]{0:T(256)} %get-tuple-element.744) | copy-start | bytes 3076
  139.1 73.4 %all-to-all-start.6 = ((bf16[128,4,256]{2,1,0:T(4,128)(2,1)}), bf16[128,4,256]{2,1,0:T(4,128)(2,1)S(1)}, u32[]{:S(2)}, u32[]{:S(2)}) async-start(bf16[128,4,256]{2,1,0:T(4,128)(2,1)} %get-tuple-element.738), calls=%async_computation.6 | async-start | bytes 524288 | tf_op jit(solution)/shard_map/all_to_all | solution.py:11
  144.8 73.4 %copy-start.9 = (s32[2048]{0:T(1024)S(1)}, s32[2048]{0:T(1024)}, u32[]{:S(2)}) copy-start(s32[2048]{0:T(1024)} %get-tuple-element.1045) | copy-start | bytes 24580
  212.5 29.4 %all-to-all-start.4 = ((bf16[128,4,256]{2,1,0:T(4,128)(2,1)}), bf16[128,4,256]{2,1,0:T(4,128)(2,1)S(1)}, u32[]{:S(2)}, u32[]{:S(2)}) async-start(bf16[128,4,256]{2,1,0:T(4,128)(2,1)} %get-tuple-element.739), calls=%async_computation.4 | async-start | bytes 524288 | tf_op jit(solution)/shard_map/all_to_all | solution.py:11
  241.9 34.6 %all-to-all-start.7 = ((f32[128,4,256]{2,1,0:T(4,128)}), f32[128,4,256]{2,1,0:T(4,128)S(1)}, u32[]{:S(2)}, u32[]{:S(2)}) async-start(f32[128,4,256]{2,1,0:T(4,128)} %reshape.88), calls=%async_computation.7 | async-start | bytes 1048576 | tf_op jit(solution)/shard_map/all_to_all | solution.py:19
  276.5 11.1 %copy-start.14 = (s32[512]{0:T(512)S(1)}, s32[512]{0:T(512)}, u32[]{:S(2)}) copy-start(s32[512]{0:T(512)} %eq.293) | copy-start | bytes 6148
  276.5 23.4 %all-to-all-start.5 = ((f32[128,4,256]{2,1,0:T(4,128)}), f32[128,4,256]{2,1,0:T(4,128)S(1)}, u32[]{:S(2)}, u32[]{:S(2)}) async-start(f32[128,4,256]{2,1,0:T(4,128)} %reshape.85), calls=%async_computation.5 | async-start | bytes 1048576 | tf_op jit(solution)/shard_map/all_to_all | solution.py:19
  286.3 157.5 %all-reduce.3.cloned.1.call-start = ((), (), s32[]{:S(2)}) async-start(), calls=%async_computation.8 | async-start | bytes 2097152 | tf_op jit(solution)/shard_map/psum | solution.py:120
Sparse Core Ops, SparseCore 0:
  293.1 150.6 all-reduce.2
where the time goes:
time: 455 us; the launch traced here: 453 us
  waiting for transfers between devices  168 us (37%)
  matrix products  88.7 us (19%)
  blocking collectives  67.1 us (15%)
  starting transfers between devices  64.9 us (14%)
  local copies, waits for them, and re-layouts  28.8 us (6%)
  other arithmetic  21.3 us (5%)
  between operations  14.5 us (3%)
    psum x1, waiting for transfers between devices, shards(): lax.psum((early_self, early_nbr, early_bias, late_self, late_nbr), ('dom'...  140 us
    dot_general x20, matrix products, tdot(): lax.dot_general(left, right, (((0,), (0,)), ((), ())), preferred_element_...  72.1 us
    psum x1, blocking collectives, shards(): lax.psum((early_self, early_nbr, early_bias, late_self, late_nbr), ('dom'...  67.1 us
    all_to_all x4, starting transfers between devices, to_masters(): lax.all_to_all(sectioned_rows, ('dom', 'sub'), split_axis=0, concat_axis=...  39.1 us
    all_to_all x4, starting transfers between devices, to_mirrors(): lax.all_to_all(picked_rows, ('dom', 'sub'), split_axis=0, concat_axis=0,...  25.8 us
    all_to_all x4, waiting for transfers between devices, to_masters(): lax.all_to_all(sectioned_rows, ('dom', 'sub'), split_axis=0, concat_axis=...  17.7 us
    lt x16, other arithmetic, one_block(): jnp.arange(block_rows, dtype=jnp.int32) + offset < live_count  10.4 us
    dot_general x4, matrix products, to_masters(): jnp.dot(placing, flat_rows, precision=lax.Precision.HIGHEST, preferred_el...  10.2 us
  transfers between devices with their start and end apart: 9, of which 4 were waited for; matrix products, arithmetic and copies ran while one was open for 25% of the time, Pallas kernels for 0%

commit v1 on v0

--- a/solution.py
+++ b/solution.py
@@ -1,8 +1,19 @@
+import functools
 import math
 import jax
 import jax.numpy as jnp
 from jax import lax
 from jax.sharding import PartitionSpec as P
+from jax.lax import psum
+
+
+def teams_close(vec, row_axis, axis_key):
+    for i in (axis_key, row_axis):
+        vec = psum(vec, i)
+    return vec
+
+
+mark_rows = functools.partial(teams_close, row_axis="sub", axis_key="dom")
 
 
 def to_mirrors(master_rows, send_list):
@@ -117,8 +128,8 @@
     grad_features = (
         dot_transposed(grad_z_one, w_self_one) + gather_sum(message_one, targets, sources)
     ).astype(jnp.bfloat16)
-    self_one, nbr_one, bias_sum, self_two, nbr_two = lax.psum(
-        (early_self, early_nbr, early_bias, late_self, late_nbr), ("dom", "sub")
+    self_one, nbr_one, bias_sum, self_two, nbr_two = mark_rows(
+        (early_self, early_nbr, early_bias, late_self, late_nbr)
     )
     norm_factor = jnp.float32(node_dev * lax.axis_size("dom") * lax.axis_size("sub")) ** (-0.5)
     grad_weights = jnp.stack([self_one, nbr_one, self_two, nbr_two]) * norm_factor

time: 455 us -> 376 us (0.83)
  waiting for transfers between devices: 168 us -> 103 us
  blocking collectives: 67.1 us -> 53.4 us
  local copies, waits for them, and re-layouts: 28.8 us -> 34.6 us
  starting transfers between devices: 64.9 us -> 59.8 us
    psum x1 -> x2, waiting for transfers between devices: 140 us -> 65.1 us  [teams_close(): vec = psum(vec, i)]
    psum x1 -> x2, blocking collectives: 67.1 us -> 53.4 us  [teams_close(): vec = psum(vec, i)]
    all_to_all x4, waiting for transfers between devices: 9.69 us -> 18.6 us  [to_mirrors(): lax.all_to_all(picked_rows, ('dom', 'sub'), split_axis=0, concat_axis=0,...]
    all_to_all x4, starting transfers between devices: 39.1 us -> 33.9 us  [to_masters(): lax.all_to_all(sectioned_rows, ('dom', 'sub'), split_axis=0, concat_axis=...]
  transfers between devices with their start and end apart: 9 -> 10, of which waited for: 4 -> 6; matrix products, arithmetic and copies ran while one was open for 25% -> 30% of each run, Pallas kernels for 0% -> 0%
where the time goes in v1:
time: 376 us; the launch traced here: 372 us
  waiting for transfers between devices  103 us (27%)
  matrix products  85.7 us (23%)
  starting transfers between devices  59.8 us (16%)
  blocking collectives  53.4 us (14%)
  local copies, waits for them, and re-layouts  34.6 us (9%)
  other arithmetic  21.2 us (6%)
  between operations  14.5 us (4%)
    dot_general x20, matrix products, tdot(): lax.dot_general(left, right, (((0,), (0,)), ((), ())), preferred_element_...  68.9 us
    psum x2, waiting for transfers between devices, teams_close(): vec = psum(vec, i)  65.1 us
    psum x2, blocking collectives, teams_close(): vec = psum(vec, i)  53.4 us
    all_to_all x4, starting transfers between devices, to_masters(): lax.all_to_all(sectioned_rows, ('dom', 'sub'), split_axis=0, concat_axis=...  33.9 us
    all_to_all x4, starting transfers between devices, to_mirrors(): lax.all_to_all(picked_rows, ('dom', 'sub'), split_axis=0, concat_axis=0,...  25.6 us
    all_to_all x4, waiting for transfers between devices, to_masters(): lax.all_to_all(sectioned_rows, ('dom', 'sub'), split_axis=0, concat_axis=...  19.1 us
    all_to_all x4, waiting for transfers between devices, to_mirrors(): lax.all_to_all(picked_rows, ('dom', 'sub'), split_axis=0, concat_axis=0,...  18.6 us
    dot_general x4, matrix products, to_masters(): jnp.dot(placing, flat_rows, precision=lax.Precision.HIGHEST, preferred_el...  10.4 us
  transfers between devices with their start and end apart: 10, of which 6 were waited for; matrix products, arithmetic and copies ran while one was open for 30% of the time, Pallas kernels for 0%

profile of v1, /device:TPU:1, one launch (start us, length us, event | category | flops | bytes accessed | tf_op | source)
XLA Modules:
  0.0 372.5 jit_solution(5858406626196903632)
XLA Ops:
  16.2 11.9 %all-to-all-start = ((bf16[128,4,256]{2,1,0:T(4,128)(2,1)}), bf16[128,4,256]{2,1,0:T(4,128)(2,1)}, u32[]{:S(2)}, u32[]{:S(2)}) async-start(bf16[128,4,256]{2,1,0:T(4,128)(2,1)} %get-tuple-element.745), calls=%async_computation | async-start | bytes 524288 | tf_op jit(solution)/shard_map/all_to_all | solution.py:22
  29.0 9.7 %all-to-all-done = bf16[128,4,256]{2,1,0:T(4,128)(2,1)} async-done(((bf16[128,4,256]{2,1,0:T(4,128)(2,1)}), bf16[128,4,256]{2,1,0:T(4,128)(2,1)}, u32[]{:S(2)}, u32[]{:S(2)}) %all-to-all-start) | async-done | bytes 262176 | tf_op jit(solution)/shard_map/all_to_all | solution.py:22
  38.7 4.6 %all-to-all-start.2 = ((bf16[128,4,256]{2,1,0:T(4,128)(2,1)}), bf16[128,4,256]{2,1,0:T(4,128)(2,1)S(1)}, u32[]{:S(2)}, u32[]{:S(2)}) async-start(bf16[128,4,256]{2,1,0:T(4,128)(2,1)} %get-tuple-element.744), calls=%async_computation.2 | async-start | bytes 524288 | tf_op jit(solution)/shard_map/all_to_all | solution.py:22
  46.9 20.3 %while.60 = (s32[]{:T(128)}, f32[1536,256]{1,0:T(8,128)S(1)}, s32[2048]{0:T(1024)S(1)}, s32[2048]{0:T(1024)}, s32[]{:T(128)}, /*index=5*/bf16[1536,256]{1,0:T(8,...) while((s32[]{:T(128)}, f32[1536,256]{1,0:T(8,128)S(1)}, s32[2048]{0:T(1024)S(1)}, ...), condition=%wide.region_1.3_spmd.clone.clone, body=%wide.region_0.0_spmd.clone.clone.sunk | while | flops 808584192 | bytes 3945645 | solution.py:64
  48.4 3.6 fusion.128
  53.5 3.6 fusion.128
  68.6 9.8 %all-to-all-start.1 = ((f32[128,4,256]{2,1,0:T(4,128)}), f32[128,4,256]{2,1,0:T(4,128)S(1)}, u32[]{:S(2)}, u32[]{:S(2)}) async-start(f32[128,4,256]{2,1,0:T(4,128)} %reshape.79), calls=%async_computation.1 | async-start | bytes 1048576 | tf_op jit(solution)/shard_map/all_to_all | solution.py:30
  78.5 22.7 %while.61 = (s32[]{:T(128)}, f32[1536,256]{1,0:T(8,128)}, s32[2048]{0:T(1024)}, s32[2048]{0:T(1024)S(1)}, s32[]{:T(128)}, /*index=5*/bf16[1536,256]{1,0:T(8,128)...) while((s32[]{:T(128)}, f32[1536,256]{1,0:T(8,128)}, s32[2048]{0:T(1024)}, ...), condition=%wide.region_3.5_spmd.clone.clone, body=%wide.region_2.4_spmd.clone.clone.sunk | while | flops 808584192 | bytes 3945645 | solution.py:64
  84.6 4.5 %fusion.131 = f32[1536,256]{1,0:T(8,128)} fusion(f32[1536,256]{1,0:T(8,128)} %get-tuple-element.909, s32[512]{0:T(512)S(1)} %dynamic_slice.82, bf16[1536,256]{1,0:T(8,128)(2,1)S(1)} %get-tuple-element.923, s32[512]{0:T(512)S(1)} %dynamic_slice.83, pred[512]{0:T(512)(128)(4,1)S(1)} %add_compare_fusion.9, pred[]{:T(512)S(6)} %compare.13), kind=kOutput, calls=%fused_computation.24.clone.1 | convolution fusion | flops 808583168 | bytes 3936769 | tf_op jit(solution)/shard_map/while/body/eval_jaxpr/dot_general | solution.py:68
  90.7 4.5 %fusion.131 = f32[1536,256]{1,0:T(8,128)} fusion(f32[1536,256]{1,0:T(8,128)} %get-tuple-element.909, s32[512]{0:T(512)S(1)} %dynamic_slice.82, bf16[1536,256]{1,0:T(8,128)(2,1)S(1)} %get-tuple-element.923, s32[512]{0:T(512)S(1)} %dynamic_slice.83, pred[512]{0:T(512)(128)(4,1)S(1)} %add_compare_fusion.9, pred[]{:T(512)S(6)} %compare.13), kind=kOutput, calls=%fused_computation.24.clone.1 | convolution fusion | flops 808583168 | bytes 3936769 | tf_op jit(solution)/shard_map/while/body/eval_jaxpr/dot_general | solution.py:68
  96.7 4.5 %fusion.131 = f32[1536,256]{1,0:T(8,128)} fusion(f32[1536,256]{1,0:T(8,128)} %get-tuple-element.909, s32[512]{0:T(512)S(1)} %dynamic_slice.82, bf16[1536,256]{1,0:T(8,128)(2,1)S(1)} %get-tuple-element.923, s32[512]{0:T(512)S(1)} %dynamic_slice.83, pred[512]{0:T(512)(128)(4,1)S(1)} %add_compare_fusion.9, pred[]{:T(512)S(6)} %compare.13), kind=kOutput, calls=%fused_computation.24.clone.1 | convolution fusion | flops 808583168 | bytes 3936769 | tf_op jit(solution)/shard_map/while/body/eval_jaxpr/dot_general | solution.py:68
  103.3 9.8 %all-to-all-start.3 = ((f32[128,4,256]{2,1,0:T(4,128)}), f32[128,4,256]{2,1,0:T(4,128)S(1)}, u32[]{:S(2)}, u32[]{:S(2)}) async-start(f32[128,4,256]{2,1,0:T(4,128)} %reshape.82), calls=%async_computation.3 | async-start | bytes 1048576 | tf_op jit(solution)/shard_map/all_to_all | solution.py:30
  117.8 8.8 %all-to-all-done.3 = f32[128,4,256]{2,1,0:T(4,128)S(1)} async-done(((f32[128,4,256]{2,1,0:T(4,128)}), f32[128,4,256]{2,1,0:T(4,128)S(1)}, u32[]{:S(2)}, u32[]{:S(2)}) %all-to-all-start.3) | async-done | bytes 524320 | tf_op jit(solution)/shard_map/all_to_all | solution.py:30
  138.9 4.6 %all-to-all-start.6 = ((bf16[128,4,256]{2,1,0:T(4,128)(2,1)}), bf16[128,4,256]{2,1,0:T(4,128)(2,1)S(1)}, u32[]{:S(2)}, u32[]{:S(2)}) async-start(bf16[128,4,256]{2,1,0:T(4,128)(2,1)} %get-tuple-element.742), calls=%async_computation.6 | async-start | bytes 524288 | tf_op jit(solution)/shard_map/all_to_all | solution.py:22
  145.7 8.9 %all-to-all-done.6 = bf16[128,4,256]{2,1,0:T(4,128)(2,1)S(1)} async-done(((bf16[128,4,256]{2,1,0:T(4,128)(2,1)}), bf16[128,4,256]{2,1,0:T(4,128)(2,1)S(1)}, u32[]{:S(2)}, u32[]{:S(2)}) %all-to-all-start.6) | async-done | bytes 262176 | tf_op jit(solution)/shard_map/all_to_all | solution.py:22
  154.6 4.5 %all-to-all-start.4 = ((bf16[128,4,256]{2,1,0:T(4,128)(2,1)}), bf16[128,4,256]{2,1,0:T(4,128)(2,1)S(1)}, u32[]{:S(2)}, u32[]{:S(2)}) async-start(bf16[128,4,256]{2,1,0:T(4,128)(2,1)} %get-tuple-element.743), calls=%async_computation.4 | async-start | bytes 524288 | tf_op jit(solution)/shard_map/all_to_all | solution.py:22
  160.1 24.4 %while.63 = (s32[]{:T(128)}, f32[1536,256]{1,0:T(8,128)}, s32[2048]{0:T(1024)}, s32[2048]{0:T(1024)S(1)}, s32[]{:T(128)}, /*index=5*/bf16[1536,256]{1,0:T(8,128)(2,1)}, s32[]{:T(128)}, s32[]{:T(128)}, s32[]{:T(128)}, s32[]{:T(128)}) while((s32[]{:T(128)}, f32[1536,256]{1,0:T(8,128)}, s32[2048]{0:T(1024)}, ...), condition=%wide.region_13.15_spmd.clone.clone, body=%wide.region_12.14_spmd.clone.clone.sunk | while | flops 808584192 | bytes 3945645 | solution.py:64
  161.6 4.2 %fusion.137 = f32[1536,256]{1,0:T(8,128)} fusion(f32[1536,256]{1,0:T(8,128)} %get-tuple-element.999, s32[512]{0:T(512)S(1)} %dynamic_slice.86, bf16[1536,256]{1,0:T(8,128)(2,1)} %get-tuple-element.1013, s32[512]{0:T(512)S(1)} %dynamic_slice.87, pred[512]{0:T(512)(128)(4,1)S(1)} %add_compare_fusion.11, pred[]{:T(512)S(6)} %compare.15), kind=kOutput, calls=%fused_computation.46.clone.1 | convolution fusion | flops 808583168 | bytes 3936769 | tf_op jit(solution)/shard_map/while/body/eval_jaxpr/dot_general | solution.py:68
  167.3 4.7 %fusion.137 = f32[1536,256]{1,0:T(8,128)} fusion(f32[1536,256]{1,0:T(8,128)} %get-tuple-element.999, s32[512]{0:T(512)S(1)} %dynamic_slice.86, bf16[1536,256]{1,0:T(8,128)(2,1)} %get-tuple-element.1013, s32[512]{0:T(512)S(1)} %dynamic_slice.87, pred[512]{0:T(512)(128)(4,1)S(1)} %add_compare_fusion.11, pred[]{:T(512)S(6)} %compare.15), kind=kOutput, calls=%fused_computation.46.clone.1 | convolution fusion | flops 808583168 | bytes 3936769 | tf_op jit(solution)/shard_map/while/body/eval_jaxpr/dot_general | solution.py:68
  173.5 4.7 %fusion.137 = f32[1536,256]{1,0:T(8,128)} fusion(f32[1536,256]{1,0:T(8,128)} %get-tuple-element.999, s32[512]{0:T(512)S(1)} %dynamic_slice.86, bf16[1536,256]{1,0:T(8,128)(2,1)} %get-tuple-element.1013, s32[512]{0:T(512)S(1)} %dynamic_slice.87, pred[512]{0:T(512)(128)(4,1)S(1)} %add_compare_fusion.11, pred[]{:T(512)S(6)} %compare.15), kind=kOutput, calls=%fused_computation.46.clone.1 | convolution fusion | flops 808583168 | bytes 3936769 | tf_op jit(solution)/shard_map/while/body/eval_jaxpr/dot_general | solution.py:68
  179.8 4.7 %fusion.137 = f32[1536,256]{1,0:T(8,128)} fusion(f32[1536,256]{1,0:T(8,128)} %get-tuple-element.999, s32[512]{0:T(512)S(1)} %dynamic_slice.86, bf16[1536,256]{1,0:T(8,128)(2,1)} %get-tuple-element.1013, s32[512]{0:T(512)S(1)} %dynamic_slice.87, pred[512]{0:T(512)(128)(4,1)S(1)} %add_compare_fusion.11, pred[]{:T(512)S(6)} %compare.15), kind=kOutput, calls=%fused_computation.46.clone.1 | convolution fusion | flops 808583168 | bytes 3936769 | tf_op jit(solution)/shard_map/while/body/eval_jaxpr/dot_general | solution.py:68
  186.5 9.8 %all-to-all-start.7 = ((f32[128,4,256]{2,1,0:T(4,128)}), f32[128,4,256]{2,1,0:T(4,128)S(1)}, u32[]{:S(2)}, u32[]{:S(2)}) async-start(f32[128,4,256]{2,1,0:T(4,128)} %reshape.88), calls=%async_computation.7 | async-start | bytes 1048576 | tf_op jit(solution)/shard_map/all_to_all | solution.py:30
  199.7 10.2 %all-to-all-done.7 = f32[128,4,256]{2,1,0:T(4,128)S(1)} async-done(((f32[128,4,256]{2,1,0:T(4,128)}), f32[128,4,256]{2,1,0:T(4,128)S(1)}, u32[]{:S(2)}, u32[]{:S(2)}) %all-to-all-start.7) | async-done | bytes 524320 | tf_op jit(solution)/shard_map/all_to_all | solution.py:30
  213.9 20.4 %while.62 = (s32[]{:T(128)}, f32[1536,256]{1,0:T(8,128)S(1)}, s32[2048]{0:T(1024)S(1)}, s32[2048]{0:T(1024)}, s32[]{:T(128)}, /*index=5*/bf16[1536,256]{1,0:T(8,...) while((s32[]{:T(128)}, f32[1536,256]{1,0:T(8,128)S(1)}, s32[2048]{0:T(1024)S(1)}, ...), condition=%wide.region_5.7_spmd.clone.clone, body=%wide.region_4.6_spmd.clone.clone.sunk | while | flops 808584192 | bytes 3945645 | solution.py:64
  215.4 3.6 fusion.134
  220.5 3.6 fusion.134
  225.6 3.6 fusion.134
  235.6 4.6 %all-to-all-start.5 = ((f32[128,4,256]{2,1,0:T(4,128)}), f32[128,4,256]{2,1,0:T(4,128)S(1)}, u32[]{:S(2)}, u32[]{:S(2)}) async-start(f32[128,4,256]{2,1,0:T(4,128)} %reshape.85), calls=%async_computation.5 | async-start | bytes 1048576 | tf_op jit(solution)/shard_map/all_to_all | solution.py:30
  240.3 34.6 %psum.78 = f32[256]{0:T(256)S(1)} all-reduce(f32[256]{0:T(256)S(1)} %copy-done.16), channel_id=1, replica_groups=mesh['dom'=16,'sub'=8] {'dom'}, use_global_device_ids=true, to_apply=%region_17.19 | all-reduce | flops 256 | bytes 2048 | tf_op jit(solution)/shard_map/psum | solution.py:12
  274.8 18.9 %psum.79 = f32[256]{0:T(256)S(1)} all-reduce(f32[256]{0:T(256)S(1)} %psum.78), channel_id=1, replica_groups=mesh['dom'=16,'sub'=8] {'sub'}, use_global_device_ids=true, to_apply=%region_18.20 | all-reduce | flops 256 | bytes 2048 | tf_op jit(solution)/shard_map/psum | solution.py:12
  294.5 4.4 %all-reduce.5.cloned.1.call-done = (f32[256,256]{0,1:T(8,128)}, f32[256,256]{0,1:T(8,128)}, f32[256,256]{0,1:T(8,128)}, f32[256,256]{0,1:T(8,128)}) async-done(((f32[256,256]{0,1:T(8,128)}, f32[256,256]{0,1:T(8,128)}, f32[256,256]{0,1:T(8,128)}, f32[256,256]{0,1:T(8,128)}), (f32[256,256]{0,1:T(8,128)}, f32[256,256]{0,1:T(8,128)}, f32[256,256]{0,1:T(8,128)}, ...) | async-done | bytes 1048592 | tf_op jit(solution)/shard_map/psum | solution.py:12
  302.3 60.7 %all-reduce.7.cloned.1.call-done = (f32[1,256,256]{1,2,0:T(8,128)}, f32[1,256,256]{1,2,0:T(8,128)}, f32[1,256,256]{1,2,0:T(8,128)}, f32[1,256,256]{1,2,0:T(8,128)}) async-done(((f32[1,256,256]{1,2,0:T(8,128)}, f32[1,256,256]{1,2,0:T(8,128)}, f32[1,256,256]{1,2,0:T(8,128)}, f32[1,256,256]{1,2,0:T(8,128)}), (f32[1,256,256]{1,2,0:T(8,128)}, f32[1,256,256]{1,2,0:T(8,128)}, f32[1,256,256]{1,2,0:T(8,128)}, ...) | async-done | bytes 1048592 | tf_op jit(solution)/shard_map/psum | solution.py:12
  (156 shorter events, 92.0 us)
Async XLA Ops:
  7.2 2.4 copy-start
  10.8 2.0 copy-start.1
  14.8 13.3 %copy-start.12 = (s32[1,128,4]{1,2,0:T(4,128)S(1)}, s32[1,128,4]{1,2,0:T(4,128)}, u32[]{:S(2)}) copy-start(s32[1,128,4]{1,2,0:T(4,128)} %param.30) | copy-start | bytes 6148
  15.0 1.2 copy-start.10
  16.2 30.7 %copy-start.9 = (s32[1,2048]{1,0:T(1,128)S(1)}, s32[1,2048]{1,0:T(1,128)}, u32[]{:S(2)}) copy-start(s32[1,2048]{1,0:T(1,128)} %param.31) | copy-start | bytes 24580
  16.2 22.5 %all-to-all-start = ((bf16[128,4,256]{2,1,0:T(4,128)(2,1)}), bf16[128,4,256]{2,1,0:T(4,128)(2,1)}, u32[]{:S(2)}, u32[]{:S(2)}) async-start(bf16[128,4,256]{2,1,0:T(4,128)(2,1)} %get-tuple-element.745), calls=%async_computation | async-start | bytes 524288 | tf_op jit(solution)/shard_map/all_to_all | solution.py:22
  38.7 29.8 %all-to-all-start.2 = ((bf16[128,4,256]{2,1,0:T(4,128)(2,1)}), bf16[128,4,256]{2,1,0:T(4,128)(2,1)S(1)}, u32[]{:S(2)}, u32[]{:S(2)}) async-start(bf16[128,4,256]{2,1,0:T(4,128)(2,1)} %get-tuple-element.744), calls=%async_computation.2 | async-start | bytes 524288 | tf_op jit(solution)/shard_map/all_to_all | solution.py:22
  67.2 1.4 copy-start.4
  68.6 34.7 %all-to-all-start.1 = ((f32[128,4,256]{2,1,0:T(4,128)}), f32[128,4,256]{2,1,0:T(4,128)S(1)}, u32[]{:S(2)}, u32[]{:S(2)}) async-start(f32[128,4,256]{2,1,0:T(4,128)} %reshape.79), calls=%async_computation.1 | async-start | bytes 1048576 | tf_op jit(solution)/shard_map/all_to_all | solution.py:30
  101.2 11.8 %copy-start.8 = (bf16[256,256]{1,0:T(8,128)(2,1)S(1)}, bf16[256,256]{1,0:T(8,128)(2,1)}, u32[]{:S(2)}) copy-start(bf16[256,256]{1,0:T(8,128)(2,1)} %param.24) | copy-start | bytes 393220
  103.3 23.4 %all-to-all-start.3 = ((f32[128,4,256]{2,1,0:T(4,128)}), f32[128,4,256]{2,1,0:T(4,128)S(1)}, u32[]{:S(2)}, u32[]{:S(2)}) async-start(f32[128,4,256]{2,1,0:T(4,128)} %reshape.82), calls=%async_computation.3 | async-start | bytes 1048576 | tf_op jit(solution)/shard_map/all_to_all | solution.py:30
  113.1 1.5 copy-start.13
  117.8 12.3 %copy-start.6 = (f32[1024,256]{1,0:T(8,128)S(1)}, f32[1024,256]{1,0:T(8,128)}, u32[]{:S(2)}) copy-start(f32[1024,256]{1,0:T(8,128)} %fusion.82) | copy-start | bytes 3145732
  117.8 12.3 %copy-start.11 = (bf16[256,256]{1,0:T(8,128)(2,1)S(1)}, bf16[256,256]{1,0:T(8,128)(2,1)}, u32[]{:S(2)}) copy-start(bf16[256,256]{1,0:T(8,128)(2,1)} %param.25) | copy-start | bytes 393220
  130.1 1.3 copy-start.7
  130.1 1.4 copy-start.5
  130.2 1.4 copy-start.17
  138.9 15.6 %all-to-all-start.6 = ((bf16[128,4,256]{2,1,0:T(4,128)(2,1)}), bf16[128,4,256]{2,1,0:T(4,128)(2,1)S(1)}, u32[]{:S(2)}, u32[]{:S(2)}) async-start(bf16[128,4,256]{2,1,0:T(4,128)(2,1)} %get-tuple-element.742), calls=%async_computation.6 | async-start | bytes 524288 | tf_op jit(solution)/shard_map/all_to_all | solution.py:22
  154.6 31.9 %all-to-all-start.4 = ((bf16[128,4,256]{2,1,0:T(4,128)(2,1)}), bf16[128,4,256]{2,1,0:T(4,128)(2,1)S(1)}, u32[]{:S(2)}, u32[]{:S(2)}) async-start(bf16[128,4,256]{2,1,0:T(4,128)(2,1)} %get-tuple-element.743), calls=%async_computation.4 | async-start | bytes 524288 | tf_op jit(solution)/shard_map/all_to_all | solution.py:22
  186.5 23.4 %all-to-all-start.7 = ((f32[128,4,256]{2,1,0:T(4,128)}), f32[128,4,256]{2,1,0:T(4,128)S(1)}, u32[]{:S(2)}, u32[]{:S(2)}) async-start(f32[128,4,256]{2,1,0:T(4,128)} %reshape.88), calls=%async_computation.7 | async-start | bytes 1048576 | tf_op jit(solution)/shard_map/all_to_all | solution.py:30
  196.3 102.6 %all-reduce.5.cloned.1.call-start = ((), (), s32[]{:S(2)}) async-start(), calls=%async_computation.8 | async-start | bytes 2097152 | tf_op jit(solution)/shard_map/psum | solution.py:12
  198.6 11.4 %copy-start.14 = (s32[512]{0:T(512)S(1)}, s32[512]{0:T(512)}, u32[]{:S(2)}) copy-start(s32[512]{0:T(512)} %eq.293) | copy-start | bytes 6148
  212.4 1.5 copy-start.2
  234.3 1.3 copy-start.3
  234.3 6.0 %copy-start.16 = (f32[256]{0:T(256)S(1)}, f32[256]{0:T(256)}, u32[]{:S(2)}) copy-start(f32[256]{0:T(256)} %get-tuple-element.748) | copy-start | bytes 3076
  235.4 63.4 %copy-start.15 = (s32[512]{0:T(512)S(1)}, s32[512]{0:T(512)}, u32[]{:S(2)}) copy-start(s32[512]{0:T(512)} %eq.293) | copy-start | bytes 6148
  235.6 58.7 %all-to-all-start.5 = ((f32[128,4,256]{2,1,0:T(4,128)}), f32[128,4,256]{2,1,0:T(4,128)S(1)}, u32[]{:S(2)}, u32[]{:S(2)}) async-start(f32[128,4,256]{2,1,0:T(4,128)} %reshape.85), calls=%async_computation.5 | async-start | bytes 1048576 | tf_op jit(solution)/shard_map/all_to_all | solution.py:30
  240.2 122.8 %all-reduce.7.cloned.1.call-start = ((), (), s32[]{:S(2)}) async-start(), calls=%async_computation.9 | async-start | bytes 2097152 | tf_op jit(solution)/shard_map/psum | solution.py:12
Sparse Core Ops, SparseCore 0:
  213.6 85.1 all-reduce.4
  301.4 61.6 all-reduce.6
